TPU v7x, 32 devices: a whole 2x2x4 slice. The times are simulated.
32 devices in a mesh: dp: 4 (over y, x), mp: 8 (over z, core).
Axes of the slice: x: 2, y: 2, z: 4, core: 2. Of those that a mesh axis runs over, the one named last changes fastest.
Arguments:
- attn_input: bfloat16 [1024, 5120], P('dp'), may hold values from -8 to 8
- attn_gain: float32 [5120], replicated, may hold values from 0.1 to 1.9
- qkv_weight: float32 [5120, 6144], P(('dp', 'mp')), may hold values from -0.2 to 0.2
- mlp_input: bfloat16 [1024, 5120], P('dp'), may hold values from -6 to 6
- mlp_gain: float32 [5120], replicated, may hold values from 0.1 to 1.9
- gate_up_weight: float32 [5120, 32768], P(('dp', 'mp')), may hold values from -0.078125 to 0.078125
- prompt_lengths: int32 [6], replicated, may hold values from 1 to 512, 1024 in all
- request_prompt: int32 [64], replicated, may hold values from 0 to 5, as said below
- page_table: int32 [64, 4], replicated, may hold values from 0 to 383, as said below
Outputs:
- attended: bfloat16 [1024, 4096], P('dp', 'mp')
- hidden: bfloat16 [1024, 16384], P('dp', 'mp')
- kv_cache: bfloat16 [384, 128, 2048], P('dp', None, 'mp')
Inputs may be any that keep to these rules, and one draw needn't show every extreme that they name: `prompt_lengths`: the lengths sum to 1024. `request_prompt`: each of the 6 prompts is named by 8 to 16 requests. `page_table`: all entries are distinct.
All inputs are finite; a program needn't handle non-finite values.
Results may differ from a plain program's by a relative error of at most 0.009.
Values may be sent and summed in bfloat16 or wider, within the bound.
No kernel may reach another device: no remote copies, remote signals or barrier semaphores. Data moves between devices by JAX's collectives and lax.ppermute only.
A program may use at most 192 MiB of HBM per device.

v0:
```python
import jax
import jax.numpy as jnp
from jax import lax
from jax.sharding import PartitionSpec as P

HEADS = 32
KVH = 8
HD = 128
PAGE = 128
SLOT_DEV = 96


EPS = 1e-05
THETA = 100000000.0


def rms_norm(stream, gain_row):
    widened = stream.astype(jnp.float32)
    squares = jnp.mean(widened * widened, axis=-1, keepdims=True)
    return (widened * lax.rsqrt(squares + EPS) * gain_row).astype(jnp.bfloat16)


def rotate(tensor, positions):
    half_dim = tensor.shape[-1] // 2
    frequency = THETA ** (-jnp.arange(half_dim, dtype=jnp.float32) / half_dim)
    angles = positions.astype(jnp.float32)[:, None] * frequency[None, :]
    cosine = jnp.cos(angles)[:, None, :]
    sine_part = jnp.sin(angles)[:, None, :]
    first_half = tensor[..., :half_dim]
    second_half = tensor[..., half_dim:]
    return jnp.concatenate(
        [
            first_half * cosine - second_half * sine_part,
            second_half * cosine + first_half * sine_part,
        ],
        axis=-1,
    )


def layout(prompt_lengths, token_ids):
    prompt_ends = jnp.cumsum(prompt_lengths)
    starts = prompt_ends - prompt_lengths
    prompt_ids = jnp.sum((token_ids[:, None] >= prompt_ends[None, :]).astype(jnp.int32), axis=1)
    matches = prompt_ids[:, None] == jnp.arange(prompt_lengths.shape[0], dtype=jnp.int32)[None, :]
    start_of = jnp.sum(jnp.where(matches, starts[None, :], 0), axis=1)
    return (prompt_ids, token_ids - start_of, starts)


def accumulate(normed, pieces):
    return tuple(
        (
            jnp.dot(normed, weight_piece, preferred_element_type=jnp.float32)
            for weight_piece in pieces
        )
    )


def feed_forward(mlp_input, mlp_gain, gate_up_weight):
    half_cols = gate_up_weight.shape[1] // 2
    server_rows = gate_up_weight.astype(jnp.bfloat16)
    gate_rows, up_rows = (
        lax.all_to_all(server_rows[:, :half_cols], "mp", split_axis=1, concat_axis=0, tiled=True),
        lax.all_to_all(server_rows[:, half_cols:], "mp", split_axis=1, concat_axis=0, tiled=True),
    )
    normed = rms_norm(mlp_input, mlp_gain)
    gate_sum, up_sum = accumulate(
        normed,
        (
            lax.all_gather(gate_rows, "dp", axis=0, tiled=True),
            lax.all_gather(up_rows, "dp", axis=0, tiled=True),
        ),
    )
    return (jax.nn.silu(gate_sum) * up_sum).astype(jnp.bfloat16)


def shards(
    attn_input,
    attn_gain,
    qkv_weight,
    mlp_input,
    mlp_gain,
    gate_up_weight,
    prompt_lengths,
    request_prompt,
    page_table,
):
    model_ways = lax.axis_size("mp")
    quarter_count = model_ways // KVH
    heads_here = HEADS // model_ways
    piece_dim = HD // quarter_count
    tok_here = attn_input.shape[0]
    server_rows = qkv_weight.astype(jnp.bfloat16)
    row_count = server_rows.shape[0]
    query_cols = HEADS * HD
    query_part = server_rows[:, :query_cols].reshape(row_count, KVH, quarter_count, heads_here * HD)
    query_part = query_part.transpose(0, 2, 1, 3).reshape(row_count, query_cols)
    key_block_cols = server_rows[:, query_cols : query_cols + KVH * HD]
    key_part = jnp.broadcast_to(
        key_block_cols[:, None, :], (row_count, quarter_count, KVH * HD)
    ).reshape(row_count, quarter_count * KVH * HD)
    value_block_cols = server_rows[:, query_cols + KVH * HD :]
    value_part = jnp.broadcast_to(
        value_block_cols[:, None, :], (row_count, quarter_count, KVH * HD)
    ).reshape(row_count, quarter_count * KVH * HD)
    query_rows, key_rows, value_rows = (
        lax.all_to_all(query_part, "mp", split_axis=1, concat_axis=0, tiled=True),
        lax.all_to_all(key_part, "mp", split_axis=1, concat_axis=0, tiled=True),
        lax.all_to_all(value_part, "mp", split_axis=1, concat_axis=0, tiled=True),
    )
    normed = rms_norm(attn_input, attn_gain)
    query_proj, key_proj, value_proj = accumulate(
        normed,
        (
            lax.all_gather(query_rows, "dp", axis=0, tiled=True),
            lax.all_gather(key_rows, "dp", axis=0, tiled=True),
            lax.all_gather(value_rows, "dp", axis=0, tiled=True),
        ),
    )
    my_quarter = lax.axis_index("mp") // KVH
    first_token = lax.axis_index("dp") * tok_here
    token_ids = first_token + jnp.arange(tok_here, dtype=jnp.int32)
    prompt_ids, positions, starts = layout(prompt_lengths, token_ids)
    queries = rotate(query_proj.reshape(tok_here, heads_here, HD), positions).astype(jnp.bfloat16)
    keys_local = rotate(key_proj[:, None, :], positions)[:, 0, :].astype(jnp.bfloat16)
    values_local = value_proj.astype(jnp.bfloat16)
    key_all, value_all = (
        lax.all_gather(keys_local, "dp", axis=0, tiled=True),
        lax.all_gather(values_local, "dp", axis=0, tiled=True),
    )
    tok_total = key_all.shape[0]
    span_len = min(tok_total // 2 + tok_here, tok_total)
    window_start = jnp.clip(first_token - tok_total // 2, 0, tok_total - span_len)
    key_block = lax.dynamic_slice_in_dim(key_all, window_start, span_len, 0)
    value_block = lax.dynamic_slice_in_dim(value_all, window_start, span_len, 0)
    key_ids = window_start + jnp.arange(span_len, dtype=jnp.int32)
    key_prompts = layout(prompt_lengths, key_ids)[0]
    scores = jnp.einsum(
        "thd,sd->hts", queries, key_block, preferred_element_type=jnp.float32
    ) * HD ** (-0.5)
    allowed = (prompt_ids[:, None] == key_prompts[None, :]) & (
        token_ids[:, None] >= key_ids[None, :]
    )
    scores = jnp.where(allowed[None], scores, -jnp.inf)
    peak = jnp.max(scores, axis=-1, keepdims=True)
    weights = jnp.exp(scores - peak)
    probs = (weights / jnp.sum(weights, axis=-1, keepdims=True)).astype(jnp.bfloat16)
    attended = jnp.einsum("hts,sd->thd", probs, value_block, preferred_element_type=jnp.float32)
    attended = attended.astype(jnp.bfloat16).reshape(tok_here, heads_here * HD)
    pages_per = page_table.shape[1]
    prompt_count = prompt_lengths.shape[0]
    slot_ids = lax.axis_index("dp") * SLOT_DEV + jnp.arange(SLOT_DEV, dtype=jnp.int32)
    flat_table = page_table.reshape(-1)
    matches = slot_ids[:, None] == flat_table[None, :]
    is_used = jnp.any(matches, axis=1)
    entry_ids = jnp.sum(
        jnp.where(matches, jnp.arange(flat_table.shape[0], dtype=jnp.int32)[None, :], 0), axis=1
    )
    request_ids = entry_ids // pages_per
    page_index = entry_ids % pages_per
    request_match = (
        request_ids[:, None] == jnp.arange(request_prompt.shape[0], dtype=jnp.int32)[None, :]
    )
    prompt_pick = jnp.sum(jnp.where(request_match, request_prompt[None, :], 0), axis=1)
    prompt_match = prompt_pick[:, None] == jnp.arange(prompt_count, dtype=jnp.int32)[None, :]
    slot_start = jnp.sum(jnp.where(prompt_match, starts[None, :], 0), axis=1)
    slot_length = jnp.sum(jnp.where(prompt_match, prompt_lengths[None, :], 0), axis=1)
    inside = page_index[:, None] * PAGE + jnp.arange(PAGE, dtype=jnp.int32)[None, :]
    valid = is_used[:, None] & (inside < slot_length[:, None])
    source = jnp.where(valid, slot_start[:, None] + inside, 0)
    key_piece = lax.dynamic_slice_in_dim(key_all, my_quarter * piece_dim, piece_dim, 1)
    value_piece = lax.dynamic_slice_in_dim(value_all, my_quarter * piece_dim, piece_dim, 1)
    page_rows = jnp.concatenate([key_piece, value_piece], axis=1)[source]
    kv_cache = jnp.where(valid[:, :, None], page_rows, jnp.zeros((), jnp.bfloat16))
    hidden = feed_forward(mlp_input, mlp_gain, gate_up_weight)
    return (attended, hidden, kv_cache)


def solution(mesh):
    placed = (
        P("dp", None),
        P(),
        P(("dp", "mp"), None),
        P("dp", None),
        P(),
        P(("dp", "mp"), None),
        P(),
        P(),
        P(),
    )
    return jax.shard_map(
        shards,
        mesh=mesh,
        in_specs=placed,
        out_specs=(P("dp", "mp"), P("dp", "mp"), P("dp", None, "mp")),
        check_vma=False,
    )
```

profile of v0, /device:TPU:0, one launch (start us, length us, event | category | flops | bytes accessed | tf_op | source)
XLA Modules:
  0.0 615.7 jit_solution(841778103808874769)
XLA Ops:
  7.2 0.0 all-gather.9.cloned.1.call-start
  7.2 2.3 convert_element_type.54
  9.6 0.1 copy.107
  9.7 17.4 %all_to_all.95 = bf16[160,8,128]{2,0,1:T(8,128)(2,1)} all-to-all(bf16[160,8,128]{2,0,1:T(8,128)(2,1)S(1)} %bitcast.95), channel_id=1, replica_groups=mesh['dp'=4,'mp'=8] {'mp'}, dimensions={1} | all-to-all | bytes 655360 | tf_op jit(solution)/shard_map/all_to_all | solution.py:107
  27.1 0.0 all-gather.9.cloned.1.call-update
  27.1 0.8 copy.108
  27.9 3.4 all-to-all-start
  31.3 0.1 slice.42
  31.4 1.2 copy.106
  32.6 12.3 %convert_element_type.65 = bf16[160,32768]{1,0:T(8,128)(2,1)} convert(f32[160,32768]{1,0:T(8,128)} %param.14) | non-fusion elementwise | flops 5242880 | bytes 31457280 | tf_op jit(solution)/shard_map/convert_element_type | solution.py:60
  44.9 5.0 all-to-all-start.2
  49.9 0.0 all-gather.7.cloned.1.call-start
  49.9 0.7 all-gather.7.cloned.1.call-update
  50.6 9.3 %fusion.62 = (bf16[160,16384]{1,0:T(8,128)(2,1)}, bf16[160,16384]{1,0:T(8,128)(2,1)}) fusion(bf16[160,32768]{1,0:T(8,128)(2,1)} %convert_element_type.65), kind=kLoop, calls=%fused_computation.102 | loop fusion | bytes 20971520 | tf_op jit(solution)/shard_map/slice | solution.py:62
  59.9 5.6 copy.105
  65.5 16.6 %all-to-all-done.2 = bf16[160,8,512]{2,0,1:T(8,128)(2,1)S(1)} async-done(((bf16[160,8,512]{2,0,1:T(8,128)(2,1)}), bf16[160,8,512]{2,0,1:T(8,128)(2,1)S(1)}, u32[]{:S(2)}, u32[]{:S(2)}) %all-to-all-start.2) | async-done | bytes 1310752 | tf_op jit(solution)/shard_map/all_to_all | solution.py:106
  82.1 1.1 copy-done
  83.2 4.7 all-to-all-start.3
  87.8 0.0 all-gather.11.cloned.1.call-start
  87.9 0.7 all-gather.11.cloned.1.call-update
  88.6 0.0 all-gather.13.cloned.1.call-start
  88.6 115.7 %all-to-all-done.3 = bf16[160,8,2048]{2,0,1:T(8,128)(2,1)} async-done(((bf16[160,8,2048]{2,0,1:T(8,128)(2,1)}), bf16[160,8,2048]{2,0,1:T(8,128)(2,1)}, u32[]{:S(2)}, u32[]{:S(2)}) %all-to-all-start.3) | async-done | bytes 5242912 | tf_op jit(solution)/shard_map/all_to_all | solution.py:62
  204.3 0.0 all-gather.13.cloned.1.call-update
  204.3 0.0 all-gather.15.cloned.1.call-start
  204.4 2.9 copy.104
  207.3 119.9 %all_to_all.96 = bf16[160,8,2048]{2,0,1:T(8,128)(2,1)} all-to-all(bf16[160,8,2048]{2,0,1:T(8,128)(2,1)S(1)} %bitcast.90), channel_id=1, replica_groups=mesh['dp'=4,'mp'=8] {'mp'}, dimensions={1} | all-to-all | bytes 10485760 | tf_op jit(solution)/shard_map/all_to_all | solution.py:63
  327.2 0.6 copy-done.12
  327.8 0.2 reduce-window.8
  328.0 0.1 copy.83
  328.1 0.1 eq.80
  328.3 0.2 fusion.32
  328.5 0.1 select_reduce_fusion
  328.6 0.2 compare_reduce_fusion
  328.8 0.1 convert_reduce_fusion.1
  328.9 0.1 select_reduce_fusion.1
  329.0 0.1 convert_reduce_fusion
  329.0 0.1 select_reduce_fusion.3
  329.1 0.6 fusion.1
  329.8 0.2 copy-done.2
  330.0 0.6 fusion.4
  330.6 0.1 fusion.44
  330.7 1.0 compare_and_fusion
  331.7 1.2 multiply_cosine_fusion
  332.9 0.7 fusion.42
  333.6 2.5 convolution_bitcast_fusion
  336.1 0.3 fusion.38
  336.4 15.1 %all-gather = bf16[1024,1,128]{0,2,1:T(8,128)(2,1)S(1)} all-gather(bf16[256,1,128]{0,2,1:T(8,128)(2,1)S(1)} %pad_maximum_fusion.2), channel_id=2, replica_groups=mesh['dp'=4,'mp'=8] {'dp'}, dimensions={0}, use_global_device_ids=true | all-gather | bytes 327680 | tf_op jit(solution)/shard_map/all_gather | solution.py:127
  351.6 2.5 convolution_convert_fusion
  354.1 14.7 %all_gather.22 = bf16[1024,128]{0,1:T(8,128)(2,1)S(1)} all-gather(bf16[256,128]{0,1:T(8,128)(2,1)S(1)} %convolution_convert_fusion), channel_id=1, replica_groups=mesh['dp'=4,'mp'=8] {'dp'}, dimensions={0}, use_global_device_ids=true | all-gather | bytes 327680 | tf_op jit(solution)/shard_map/all_gather | solution.py:128
  368.7 0.7 copy-done.5
  369.4 0.8 pad_maximum_fusion
  370.3 1.2 copy.84
  371.5 53.2 %gather_fusion = bf16[12288,256]{1,0:T(8,128)(2,1)} fusion(bf16[1024,256]{1,0:T(8,128)(2,1)S(1)} %copy.84, s32[12288]{0:T(1024)} %fusion.42), kind=kCustom, calls=%fused_computation | custom fusion | bytes 12632064 | tf_op jit(solution)/shard_map/gather | solution.py:172
  424.7 7.6 %broadcast_select_fusion = bf16[96,128,256]{2,1,0:T(8,128)(2,1)} fusion(bf16[96,128,256]{2,1,0:T(8,128)(2,1)} %bitcast.85, pred[96,128]{1,0:T(8,128)(4,1)S(1)} %fusion.44), kind=kLoop, calls=%fused_computation.6 | loop fusion | flops 3145728 | bytes 12595200 | tf_op jit(solution)/shard_map/jit(_where)/select_n | solution.py:173
  432.3 4.8 fusion.58
  437.1 1.3 reshape.447
  438.4 0.3 fusion.63
  438.7 0.1 subtract_convert_fusion
  438.9 3.1 fusion.64
  442.0 2.5 fusion.13
  444.5 0.8 copy.85
  445.3 11.3 %fusion.15 = f32[256,2048]{1,0:T(8,128)} fusion(bf16[5120,2048]{1,0:T(8,128)(2,1)} %all-gather.13.cloned.1.call-done, bf16[256,5120]{1,0:T(8,128)(2,1)S(1)} %copy-done.3, f32[5120]{0:T(1024)S(1)} %copy-done.15, f32[256]{0:T(256)S(1)} %add_rsqrt_fusion), kind=kOutput, calls=%fused_computation.30 | convolution fusion | flops 5373952000 | bytes 25711616 | tf_op jit(solution)/shard_map/dot_general | solution.py:52
  456.6 140.5 %all-gather.15.cloned.1.call-done = bf16[5120,2048]{1,0:T(8,128)(2,1)} async-done(((bf16[1280,2048]{1,0:T(8,128)(2,1)}), bf16[5120,2048]{1,0:T(8,128)(2,1)}) %all-gather.15.cloned.1.call-update) | async-done | bytes 20971536 | tf_op jit(solution)/shard_map/all_gather | solution.py:70
  597.1 12.0 %fusion.7 = bf16[256,2048]{1,0:T(8,128)(2,1)} fusion(bf16[5120,2048]{1,0:T(8,128)(2,1)} %all-gather.15.cloned.1.call-done, f32[256,2048]{1,0:T(8,128)} %fusion.15, bf16[256,5120]{1,0:T(8,128)(2,1)S(1)} %copy-done.3, f32[5120]{0:T(1024)S(1)} %copy-done.15, f32[256]{0:T(256)S(1)} %add_rsqrt_fusion), kind=kOutput, calls=%fused_computation.19 | convolution fusion | flops 5377097728 | bytes 26760192 | tf_op jit(solution)/shard_map/dot_general | solution.py:52
  (47 shorter events, 0.2 us)
Async XLA Ops:
  7.2 326.5 %all-gather.9.cloned.1.call-start = ((), (), s32[]{:S(2)}) async-start(), calls=%async_computation.6 | async-start | bytes 1638400 | tf_op jit(solution)/shard_map/all_gather | solution.py:115
  27.9 17.0 %all-to-all-start = ((bf16[160,8,128]{2,0,1:T(8,128)(2,1)}), bf16[160,8,128]{2,0,1:T(8,128)(2,1)S(1)}, u32[]{:S(2)}, u32[]{:S(2)}) async-start(bf16[160,8,128]{2,0,1:T(8,128)(2,1)} %bitcast.84), calls=%async_computation | async-start | bytes 655360 | tf_op jit(solution)/shard_map/all_to_all | solution.py:108
  44.9 5.1 copy-start.4
  44.9 37.2 %all-to-all-start.2 = ((bf16[160,8,512]{2,0,1:T(8,128)(2,1)}), bf16[160,8,512]{2,0,1:T(8,128)(2,1)S(1)}, u32[]{:S(2)}, u32[]{:S(2)}) async-start(bf16[160,8,512]{2,0,1:T(8,128)(2,1)} %bitcast.82), calls=%async_computation.2 | async-start | bytes 2621440 | tf_op jit(solution)/shard_map/all_to_all | solution.py:106
  49.9 301.7 %all-gather.7.cloned.1.call-start = ((), (), s32[]{:S(2)}) async-start(), calls=%async_computation.5 | async-start | bytes 1638400 | tf_op jit(solution)/shard_map/all_gather | solution.py:116
  82.1 1.1 copy-start
  83.2 121.1 %all-to-all-start.3 = ((bf16[160,8,2048]{2,0,1:T(8,128)(2,1)}), bf16[160,8,2048]{2,0,1:T(8,128)(2,1)}, u32[]{:S(2)}, u32[]{:S(2)}) async-start(bf16[160,8,2048]{2,0,1:T(8,128)(2,1)} %bitcast.89), calls=%async_computation.3 | async-start | bytes 10485760 | tf_op jit(solution)/shard_map/all_to_all | solution.py:62
  87.8 344.5 %all-gather.11.cloned.1.call-start = ((), (), s32[]{:S(2)}) async-start(), calls=%async_computation.7 | async-start | bytes 6553600 | tf_op jit(solution)/shard_map/all_gather | solution.py:114
  88.6 356.8 %all-gather.13.cloned.1.call-start = ((), (), s32[]{:S(2)}) async-start(), calls=%async_computation.8 | async-start | bytes 26214400 | tf_op jit(solution)/shard_map/all_gather | solution.py:69
  204.3 392.8 %all-gather.15.cloned.1.call-start = ((), (), s32[]{:S(2)}) async-start(), calls=%async_computation.9 | async-start | bytes 26214400 | tf_op jit(solution)/shard_map/all_gather | solution.py:70
  327.2 0.7 copy-start.12
  327.2 0.8 copy-start.9
  327.2 1.3 copy-start.16
  327.2 1.9 copy-start.1
  327.2 6.4 %copy-start.13 = (f32[5120]{0:T(1024)S(1)}, f32[5120]{0:T(1024)}, u32[]{:S(2)}) copy-start(f32[5120]{0:T(1024)} %param.10) | copy-start | bytes 61444
  328.2 1.7 copy-start.2
  330.0 21.6 %copy-start.10 = (f32[256]{0:T(256)}, f32[256]{0:T(256)S(1)}, u32[]{:S(2)}) copy-start(f32[256]{0:T(256)S(1)} %add_rsqrt_fusion.1) | copy-start | bytes 3076
  368.7 0.7 copy-start.5
  424.7 7.6 %copy-start.11 = (f32[256]{0:T(256)S(1)}, f32[256]{0:T(256)}, u32[]{:S(2)}) copy-start(f32[256]{0:T(256)} %copy-done.10) | copy-start | bytes 3076
  424.7 7.6 %copy-start.14 = (f32[5120]{0:T(1024)S(1)}, f32[5120]{0:T(1024)}, u32[]{:S(2)}) copy-start(f32[5120]{0:T(1024)} %param.10) | copy-start | bytes 61444
  437.1 1.6 copy-start.7
  437.1 1.8 copy-start.8
  438.9 3.1 copy-start.6
  442.0 3.3 copy-start.3
  442.0 3.3 copy-start.15
Sparse Core Ops, SparseCore 0:
  27.2 27.7 all-gather.8
  57.4 28.7 all-gather.6
  90.5 62.7 all-gather.10
  204.4 197.6 all-gather.12
  403.9 193.1 all-gather.14
where the time goes:
time: 618 us; the launch traced here: 616 us
  waiting for transfers between devices  274 us (44%)
  blocking collectives  167 us (27%)
  local copies, waits for them, and re-layouts  79.6 us (13%)
  matrix products  38.7 us (6%)
  other arithmetic  28.7 us (5%)
  between operations  14.1 us (2%)
  starting transfers between devices  13.3 us (2%)
    all_gather x1, waiting for transfers between devices, feed_forward(): lax.all_gather(up_rows, 'dp', axis=0, tiled=True)  140 us
    all_to_all x1, blocking collectives, feed_forward(): lax.all_to_all(server_rows[:, half_cols:], 'mp', split_axis=1, concat_axi...  120 us
    all_to_all x1, waiting for transfers between devices, feed_forward(): lax.all_to_all(server_rows[:, :half_cols], 'mp', split_axis=1, concat_axi...  116 us
    gather x1, local copies, waits for them, and re-layouts, shards(): page_rows = jnp.concatenate([key_piece, value_piece], axis=1)[source]  53.2 us
    dot_general x5, matrix products, accumulate(): jnp.dot(normed, weight_piece, preferred_element_type=jnp.float32)  33.1 us
    all_to_all x1, blocking collectives, shards(): lax.all_to_all(key_part, 'mp', split_axis=1, concat_axis=0, tiled=True)  17.4 us
    all_to_all x1, waiting for transfers between devices, shards(): lax.all_to_all(query_part, 'mp', split_axis=1, concat_axis=0, tiled=True)  16.6 us
    all_gather x1, blocking collectives, shards(): lax.all_gather(keys_local, 'dp', axis=0, tiled=True)  15.1 us
  transfers between devices with their start and end apart: 8, of which 3 were waited for; matrix products, arithmetic and copies ran while one was open for 21% of the time, Pallas kernels for 0%

commit v1 on v0

v1 whole, which is shorter than its diff:
```python
import functools

import jax
import jax.numpy as jnp
from jax import lax
from jax.experimental import pallas as pl
from jax.experimental.pallas import tpu as pltpu
from jax.sharding import PartitionSpec as P

HEADS = 32
KVH = 8
HD = 128
PAGE = 128
EPS = 1e-05
THETA = 100000000.0
CHUNKS = 4
SLOT_DEV = 96
SLOT_GROUP = 8


def rms_norm(stream, gain_row):
    widened = stream.astype(jnp.float32)
    squares = jnp.mean(widened * widened, axis=-1, keepdims=True)
    return (widened * lax.rsqrt(squares + EPS) * gain_row).astype(jnp.bfloat16)


def rotate(tensor, positions):
    half_dim = tensor.shape[-1] // 2
    frequency = THETA ** (-jnp.arange(half_dim, dtype=jnp.float32) / half_dim)
    angles = positions.astype(jnp.float32)[:, None] * frequency[None, :]
    cosine = jnp.cos(angles)[:, None, :]
    sine_part = jnp.sin(angles)[:, None, :]
    first_half = tensor[..., :half_dim]
    second_half = tensor[..., half_dim:]
    return jnp.concatenate(
        [
            first_half * cosine - second_half * sine_part,
            second_half * cosine + first_half * sine_part,
        ],
        axis=-1,
    )


def swap(value, axis, offset):
    ways = lax.axis_size(axis)
    return lax.ppermute(value, axis, [(i, i ^ offset) for i in range(ways)])


def bits_of(ways):
    return [1 << i for i in range(ways.bit_length() - 1)]


def exchange_tokens(normed, rows):
    data_ways = lax.axis_size("dp")
    group = lax.axis_size("mp") // 2
    data_at, model_at = lax.axis_index("dp"), lax.axis_index("mp")
    tokens = normed.shape[0]
    half = lax.dynamic_index_in_dim(
        normed.reshape(tokens, data_ways, 2, group * rows), model_at // group, 2, keepdims=False
    )
    cells = half.reshape(tokens, data_ways, group, rows)
    for bit in bits_of(group):
        view = cells.reshape(tokens, data_ways, group // (2 * bit), 2, bit, rows)
        cells = jnp.where((model_at & bit) != 0, view[:, :, :, ::-1], view).reshape(cells.shape)
    cells = cells.transpose(1, 0, 2, 3).reshape(data_ways, tokens, group * rows)
    blocks = []
    for s in range(data_ways):
        block = lax.dynamic_index_in_dim(cells, data_at ^ s, 0, keepdims=False)
        blocks.append(block if s == 0 else swap(block, "dp", s))
    return blocks


def exchange_weights(pack):
    group = lax.axis_size("mp") // 2
    model_at = lax.axis_index("mp")
    side, member = model_at // group, model_at % group
    packets = []
    for s in range(group):
        packet = jnp.concatenate(
            [pack((side ^ a) * group + (member ^ s)) for a in range(2)], axis=1
        )
        packets.append(packet if s == 0 else swap(packet, "mp", s))
    width = packets[0].shape[1] // 2
    return [
        jnp.concatenate([packet[:, a * width : (a + 1) * width] for packet in packets], axis=0)
        for a in range(2)
    ]


def scattered_product(blocks, weights, order):
    arrived = {s: [] for s in range(len(blocks))}
    remaining = list(range(len(blocks)))

    def product(which):
        left = blocks[which[0]] if len(which) == 1 else jnp.concatenate([blocks[s] for s in which])
        total = jnp.dot(left, weights, preferred_element_type=jnp.float32)
        for parts in zip(*[arrived[s] for s in which]):
            joined = parts[0] if len(which) == 1 else jnp.concatenate(parts)
            total = total + joined.astype(jnp.float32)
        return total

    for bit in order:
        leaving = [s for s in remaining if s & bit]
        remaining = [s for s in remaining if not s & bit]
        received = swap(product(leaving).astype(jnp.bfloat16), "dp", bit)
        tokens = received.shape[0] // len(leaving)
        for i, s in enumerate(leaving):
            arrived[s ^ bit].append(received[i * tokens : (i + 1) * tokens])
    return product([0])


def projected(blocks, pack):
    own, other = exchange_weights(pack)
    order = bits_of(len(blocks))
    far = scattered_product(blocks, other, order[::-1]).astype(jnp.bfloat16)
    near = scattered_product(blocks, own, order)
    return near + swap(far, "mp", lax.axis_size("mp") // 2).astype(jnp.float32)


def feed_forward(blocks, gate_up_weight):
    ways = lax.axis_size("mp")
    half_cols = gate_up_weight.shape[1] // 2
    cols = half_cols // ways
    width = cols // CHUNKS
    pieces = []
    for chunk in range(CHUNKS):

        def pack(device):
            start = device * cols + chunk * width
            gate = lax.dynamic_slice_in_dim(gate_up_weight, start, width, 1)
            up = lax.dynamic_slice_in_dim(gate_up_weight, half_cols + start, width, 1)
            return jnp.concatenate([gate, up], axis=1).astype(jnp.bfloat16)

        both = projected(blocks, pack)
        pieces.append((jax.nn.silu(both[:, :width]) * both[:, width:]).astype(jnp.bfloat16))
    return jnp.concatenate(pieces, axis=1)


def attend_kernel(q_ref, k_ref, v_ref, first_ref, token_ref, out_ref):
    scores = lax.dot_general(
        q_ref[...], k_ref[...], (((1,), (1,)), ((), ())), preferred_element_type=jnp.float32
    ) * HD ** (-0.5)
    key_ids = lax.broadcasted_iota(jnp.int32, scores.shape, 1)
    allowed = (key_ids >= first_ref[...]) & (key_ids <= token_ref[...])
    scores = jnp.where(allowed, scores, -jnp.inf)
    peak = jnp.max(scores, axis=-1, keepdims=True)
    weights = jnp.exp(scores - peak)
    probs = (weights / jnp.sum(weights, axis=-1, keepdims=True)).astype(jnp.bfloat16)
    out_ref[...] = jnp.dot(probs, v_ref[...], preferred_element_type=jnp.float32).astype(jnp.bfloat16)


def attend(queries, keys, values, first, token):
    tokens, width = queries.shape
    total = keys.shape[0]
    heads = width // HD
    return pl.pallas_call(
        attend_kernel,
        grid=(heads,),
        in_specs=[
            pl.BlockSpec((tokens, HD), lambda h: (0, h)),
            pl.BlockSpec((total, HD), lambda h: (0, 0)),
            pl.BlockSpec((total, HD), lambda h: (0, 0)),
            pl.BlockSpec((tokens, 1), lambda h: (0, 0)),
            pl.BlockSpec((tokens, 1), lambda h: (0, 0)),
        ],
        out_specs=pl.BlockSpec((tokens, HD), lambda h: (0, h)),
        out_shape=jax.ShapeDtypeStruct((tokens, width), jnp.bfloat16),
        cost_estimate=pl.CostEstimate(
            flops=4 * tokens * total * width,
            transcendentals=tokens * total * heads,
            bytes_accessed=4 * tokens * width + 4 * total * HD,
        ),
        name="attend",
    )(queries, keys, values, first, token)


def pages_kernel(start_ref, count_ref, rows_ref, out_ref):
    group = out_ref.shape[0]
    base = pl.program_id(0) * group
    for i in range(group):
        start = start_ref[base + i]
        shift = lax.rem(start, 8)
        tall = rows_ref[pl.ds(pl.multiple_of(start - shift, 8), PAGE + 8), :]
        page = pltpu.roll(tall, lax.rem(PAGE + 8 - shift, PAGE + 8), 0)[:PAGE]
        inside = lax.broadcasted_iota(jnp.int32, page.shape, 0)
        out_ref[i] = jnp.where(inside < count_ref[base + i], page, 0.0).astype(jnp.bfloat16)


def fill_pages(rows, start, count):
    slots, width = start.shape[0], rows.shape[1]
    padded = jnp.concatenate(
        [rows.astype(jnp.float32), jnp.zeros((PAGE, width), jnp.float32)], axis=0
    )
    return pl.pallas_call(
        pages_kernel,
        grid_spec=pltpu.PrefetchScalarGridSpec(
            num_scalar_prefetch=2,
            grid=(slots // SLOT_GROUP,),
            in_specs=[pl.BlockSpec(padded.shape, lambda i, s, c: (0, 0))],
            out_specs=pl.BlockSpec((SLOT_GROUP, PAGE, width), lambda i, s, c: (i, 0, 0)),
        ),
        out_shape=jax.ShapeDtypeStruct((slots, PAGE, width), jnp.bfloat16),
        cost_estimate=pl.CostEstimate(
            flops=slots * PAGE * width,
            transcendentals=0,
            bytes_accessed=2 * slots * PAGE * width + 4 * padded.size,
        ),
        name="fill_pages",
    )(start, count, padded)


def page_sources(prompt_lengths, starts, request_prompt, page_table, slots):
    pages_per = page_table.shape[1]
    slot_ids = lax.axis_index("dp") * slots + jnp.arange(slots, dtype=jnp.int32)
    flat_table = page_table.reshape(-1)
    matches = slot_ids[:, None] == flat_table[None, :]
    is_used = jnp.any(matches, axis=1)
    entry_ids = jnp.sum(
        jnp.where(matches, jnp.arange(flat_table.shape[0], dtype=jnp.int32)[None, :], 0), axis=1
    )
    request_ids = entry_ids // pages_per
    offset = (entry_ids % pages_per) * PAGE
    request_match = (
        request_ids[:, None] == jnp.arange(request_prompt.shape[0], dtype=jnp.int32)[None, :]
    )
    prompt_pick = jnp.sum(jnp.where(request_match, request_prompt[None, :], 0), axis=1)
    prompt_match = (
        prompt_pick[:, None] == jnp.arange(prompt_lengths.shape[0], dtype=jnp.int32)[None, :]
    )
    slot_start = jnp.sum(jnp.where(prompt_match, starts[None, :], 0), axis=1)
    slot_length = jnp.sum(jnp.where(prompt_match, prompt_lengths[None, :], 0), axis=1)
    count = jnp.where(is_used, jnp.clip(slot_length - offset, 0, PAGE), 0)
    return jnp.where(count > 0, slot_start + offset, 0), count


def shards(
    attn_input,
    attn_gain,
    qkv_weight,
    mlp_input,
    mlp_gain,
    gate_up_weight,
    prompt_lengths,
    request_prompt,
    page_table,
    *,
    slots,
):
    model_ways = lax.axis_size("mp")
    quarter_count = model_ways // KVH
    heads_here = HEADS // model_ways
    piece_dim = HD // quarter_count
    tok_here = attn_input.shape[0]
    rows = qkv_weight.shape[0]
    query_width = heads_here * HD
    query_cols = HEADS * HD

    attn_blocks = exchange_tokens(rms_norm(attn_input, attn_gain), rows)
    mlp_blocks = exchange_tokens(rms_norm(mlp_input, mlp_gain), rows)

    def pack(device):
        kv_head, quarter = device % KVH, device // KVH
        query = lax.dynamic_slice_in_dim(
            qkv_weight, (kv_head * quarter_count + quarter) * query_width, query_width, 1
        )
        key = lax.dynamic_slice_in_dim(qkv_weight, query_cols + kv_head * HD, HD, 1)
        value = lax.dynamic_slice_in_dim(qkv_weight, query_cols + (KVH + kv_head) * HD, HD, 1)
        return jnp.concatenate([query, key, value], axis=1).astype(jnp.bfloat16)

    heads = projected(attn_blocks, pack).reshape(tok_here, heads_here + 2, HD)

    first_token = lax.axis_index("dp") * tok_here
    token_ids = first_token + jnp.arange(tok_here, dtype=jnp.int32)
    prompt_ends = jnp.cumsum(prompt_lengths)
    starts = prompt_ends - prompt_lengths
    begun = token_ids[:, None] >= starts[None, :]
    first = jnp.max(jnp.where(begun, starts[None, :], 0), axis=1)
    turned = rotate(heads[:, : heads_here + 1], token_ids - first).astype(jnp.bfloat16)
    queries = turned[:, :heads_here].reshape(tok_here, query_width)
    kv_local = jnp.concatenate(
        [turned[:, heads_here], heads[:, heads_here + 1].astype(jnp.bfloat16)], axis=1
    )
    kv_all = lax.all_gather(kv_local, "dp", axis=0, tiled=True)
    attended = attend(
        queries, kv_all[:, :HD], kv_all[:, HD:], first[:, None], token_ids[:, None]
    )
    piece_at = (lax.axis_index("mp") // KVH) * piece_dim
    page_rows = jnp.concatenate(
        [
            lax.dynamic_slice_in_dim(kv_all, piece_at, piece_dim, 1),
            lax.dynamic_slice_in_dim(kv_all, HD + piece_at, piece_dim, 1),
        ],
        axis=1,
    )
    kv_cache = fill_pages(
        page_rows, *page_sources(prompt_lengths, starts, request_prompt, page_table, slots)
    )
    hidden = feed_forward(mlp_blocks, gate_up_weight)
    return (attended, hidden, kv_cache)


def solution(mesh):
    data_ways = mesh.shape["dp"]
    placed = (
        P("dp", None),
        P(),
        P(("dp", "mp"), None),
        P("dp", None),
        P(),
        P(("dp", "mp"), None),
        P(),
        P(),
        P(),
    )

    def run(*args):
        return jax.shard_map(
            functools.partial(shards, slots=SLOT_DEV),
            mesh=mesh,
            in_specs=placed,
            out_specs=(P("dp", "mp"), P("dp", "mp"), P("dp", None, "mp")),
            check_vma=False,
        )(*args)

    return run
```

time: 618 us -> 468 us (0.76)
  blocking collectives: 167 us -> 29.6 us
  starting transfers between devices: 13.3 us -> 53.2 us
  waiting for transfers between devices: 274 us -> 238 us
  local copies, waits for them, and re-layouts: 79.6 us -> 56.8 us
  Pallas kernels: 0 us -> 15.2 us
  between operations: 14.1 us -> 2.85 us
    ppermute x0 -> x46, waiting for transfers between devices: none -> 238 us  [swap(): return lax.ppermute(value, axis, [(i, i ^ offset) for i in range(ways)])]
    all_gather x5 -> x0, waiting for transfers between devices: 140 us -> none  [the longest x1 140 us: feed_forward(): lax.all_gather(up_rows, 'dp', axis=0, tiled=True)]
    all_to_all x2 -> x0, blocking collectives: 137 us -> none  [the longest x1 120 us: feed_forward(): lax.all_to_all(server_rows[:, half_cols:], 'mp', split_axis=1, concat_axi...]
    all_to_all x3 -> x0, waiting for transfers between devices: 132 us -> none  [the longest x1 116 us: feed_forward(): lax.all_to_all(server_rows[:, :half_cols], 'mp', split_axis=1, concat_axi...]
    ppermute x0 -> x46, starting transfers between devices: none -> 53.2 us  [swap(): return lax.ppermute(value, axis, [(i, i ^ offset) for i in range(ways)])]
    gather x1 -> x0, local copies, waits for them, and re-layouts: 53.2 us -> none  [shards(): page_rows = jnp.concatenate([key_piece, value_piece], axis=1)[source]]
    another operation x0 -> x6, local copies, waits for them, and re-layouts: none -> 18.5 us  [run(): jax.shard_map(functools.partial(shards, slots=SLOT_DEV), mesh=mesh, in_sp...]
    unnamed x37 -> x274, local copies, waits for them, and re-layouts: 3.62 us -> 19.6 us
  transfers between devices with their start and end apart: 8 -> 46, of which waited for: 3 -> 19; matrix products, arithmetic and copies ran while one was open for 21% -> 23% of each run, Pallas kernels for 0% -> 3%
where the time goes in v1:
time: 468 us; the launch traced here: 466 us
  waiting for transfers between devices  238 us (51%)
  local copies, waits for them, and re-layouts  56.8 us (12%)
  starting transfers between devices  53.2 us (11%)
  matrix products  43.5 us (9%)
  blocking collectives  29.6 us (6%)
  other arithmetic  27.1 us (6%)
  Pallas kernels  15.2 us (3%)
    ppermute x46, waiting for transfers between devices, swap(): return lax.ppermute(value, axis, [(i, i ^ offset) for i in range(ways)])  238 us
    ppermute x46, starting transfers between devices, swap(): return lax.ppermute(value, axis, [(i, i ^ offset) for i in range(ways)])  53.2 us
    dot_general x30, matrix products, product(): total = jnp.dot(left, weights, preferred_element_type=jnp.float32)  43.5 us
    all_gather x1, blocking collectives, shards(): kv_all = lax.all_gather(kv_local, 'dp', axis=0, tiled=True)  29.6 us
    unnamed x274, local copies, waits for them, and re-layouts  19.6 us
    another operation x6, local copies, waits for them, and re-layouts, run(): jax.shard_map(functools.partial(shards, slots=SLOT_DEV), mesh=mesh, in_sp...  18.5 us
    concatenate x12, other arithmetic, exchange_weights(): jnp.concatenate([pack((side ^ a) * group + (member ^ s)) for a in range(2...  11.1 us
    dynamic_slice x8, local copies, waits for them, and re-layouts, exchange_tokens(): block = lax.dynamic_index_in_dim(cells, data_at ^ s, 0, keepdims=False)  11.1 us
  transfers between devices with their start and end apart: 46, of which 19 were waited for; matrix products, arithmetic and copies ran while one was open for 23% of the time, Pallas kernels for 3%

profile of v1, /device:TPU:0, one launch (start us, length us, event | category | flops | bytes accessed | tf_op | source)
XLA Modules:
  0.0 466.0 jit_solution(5745307969567590364)
XLA Ops:
  0.7 3.0 copy.58
  5.1 3.0 copy.46
  8.9 4.5 fusion.5
  13.4 2.3 fusion.2
  17.4 1.9 copy.48
  19.2 2.9 collective-permute-start.3
  22.2 1.9 fusion.61
  24.1 1.6 constant_dynamic-update-slice_fusion.3
  25.7 1.6 constant_dynamic-update-slice_fusion.2
  27.3 2.2 dynamic-slice_convert_fusion.71
  29.5 1.6 constant_dynamic-update-slice_fusion.1
  31.1 1.8 dynamic-slice_convert_fusion.87
  35.5 1.9 copy.60
  37.8 1.9 copy.61
  39.7 2.6 collective-permute-start.15
  42.2 1.9 copy.62
  47.2 3.9 dynamic-slice_convert_fusion.63
  53.8 3.9 dynamic-slice_convert_fusion.62
  60.5 3.9 dynamic-slice_convert_fusion.49
  68.1 2.8 dynamic-slice_convert_fusion.61
  79.2 1.6 collective-permute-start.1
  84.8 7.5 %collective-permute-done.1 = bf16[160,1536]{1,0:T(8,128)(2,1)S(1)} collective-permute-done((bf16[160,1536]{1,0:T(8,128)(2,1)}, bf16[160,1536]{1,0:T(8,128)(2,1)S(1)}, u32[]{:S(2)}, u32[]{:S(2)}) %collective-permute-start.1) | collective-permute-done | bytes 491552 | tf_op jit(solution)/shard_map/ppermute | solution.py:46
  97.2 1.9 convolution_convert_fusion.9
  99.1 10.2 %collective-permute-done.40 = bf16[160,2048]{1,0:T(8,128)(2,1)S(1)} collective-permute-done((bf16[160,2048]{1,0:T(8,128)(2,1)S(1)}, bf16[160,2048]{1,0:T(8,128)(2,1)S(1)}, u32[]{:S(2)}, u32[]{:S(2)}) %collective-permute-start.40) | collective-permute-done | bytes 655392 | tf_op jit(solution)/shard_map/ppermute | solution.py:46
  109.4 12.1 %collective-permute-done.39 = bf16[160,2048]{1,0:T(8,128)(2,1)S(1)} collective-permute-done((bf16[160,2048]{1,0:T(8,128)(2,1)S(1)}, bf16[160,2048]{1,0:T(8,128)(2,1)S(1)}, u32[]{:S(2)}, u32[]{:S(2)}) %collective-permute-start.39) | collective-permute-done | bytes 655392 | tf_op jit(solution)/shard_map/ppermute | solution.py:46
  121.5 1.9 collective-permute-start.24
  125.1 12.3 %collective-permute-done.32 = bf16[160,2048]{1,0:T(8,128)(2,1)S(1)} collective-permute-done((bf16[160,2048]{1,0:T(8,128)(2,1)S(1)}, bf16[160,2048]{1,0:T(8,128)(2,1)S(1)}, u32[]{:S(2)}, u32[]{:S(2)}) %collective-permute-start.32) | collective-permute-done | bytes 655392 | tf_op jit(solution)/shard_map/ppermute | solution.py:46
  137.5 12.1 %collective-permute-done.31 = bf16[160,2048]{1,0:T(8,128)(2,1)S(1)} collective-permute-done((bf16[160,2048]{1,0:T(8,128)(2,1)S(1)}, bf16[160,2048]{1,0:T(8,128)(2,1)S(1)}, u32[]{:S(2)}, u32[]{:S(2)}) %collective-permute-start.31) | collective-permute-done | bytes 655392 | tf_op jit(solution)/shard_map/ppermute | solution.py:46
  149.5 1.9 collective-permute-start.13
  153.1 12.3 %collective-permute-done.24 = bf16[160,2048]{1,0:T(8,128)(2,1)S(1)} collective-permute-done((bf16[160,2048]{1,0:T(8,128)(2,1)S(1)}, bf16[160,2048]{1,0:T(8,128)(2,1)S(1)}, u32[]{:S(2)}, u32[]{:S(2)}) %collective-permute-start.24) | collective-permute-done | bytes 655392 | tf_op jit(solution)/shard_map/ppermute | solution.py:46
  165.6 12.1 %collective-permute-done.23 = bf16[160,2048]{1,0:T(8,128)(2,1)S(1)} collective-permute-done((bf16[160,2048]{1,0:T(8,128)(2,1)S(1)}, bf16[160,2048]{1,0:T(8,128)(2,1)S(1)}, u32[]{:S(2)}, u32[]{:S(2)}) %collective-permute-start.23) | collective-permute-done | bytes 655392 | tf_op jit(solution)/shard_map/ppermute | solution.py:46
  180.9 12.7 %collective-permute-done.13 = bf16[160,2048]{1,0:T(8,128)(2,1)S(1)} collective-permute-done((bf16[160,2048]{1,0:T(8,128)(2,1)S(1)}, bf16[160,2048]{1,0:T(8,128)(2,1)S(1)}, u32[]{:S(2)}, u32[]{:S(2)}) %collective-permute-start.13) | collective-permute-done | bytes 655392 | tf_op jit(solution)/shard_map/ppermute | solution.py:46
  196.4 9.2 %collective-permute-done.12 = bf16[160,2048]{1,0:T(8,128)(2,1)S(1)} collective-permute-done((bf16[160,2048]{1,0:T(8,128)(2,1)S(1)}, bf16[160,2048]{1,0:T(8,128)(2,1)S(1)}, u32[]{:S(2)}, u32[]{:S(2)}) %collective-permute-start.12) | collective-permute-done | bytes 655392 | tf_op jit(solution)/shard_map/ppermute | solution.py:46
  212.3 1.5 fusion.37
  217.5 22.5 %collective-permute-done.9 = bf16[256,768]{1,0:T(8,128)(2,1)S(1)} collective-permute-done((bf16[256,768]{1,0:T(8,128)(2,1)S(1)}, bf16[256,768]{1,0:T(8,128)(2,1)S(1)}, u32[]{:S(2)}, u32[]{:S(2)}) %collective-permute-start.9) | collective-permute-done | bytes 393248 | tf_op jit(solution)/shard_map/ppermute | solution.py:46
  242.6 2.3 fusion.27
  244.9 1.6 collective-permute-start.19
  246.5 2.4 fusion.26
  249.5 2.4 fusion.25
  251.9 10.5 %collective-permute-done.33 = bf16[512,1024]{1,0:T(8,128)(2,1)S(1)} collective-permute-done((bf16[512,1024]{1,0:T(8,128)(2,1)S(1)}, bf16[512,1024]{1,0:T(8,128)(2,1)S(1)}, u32[]{:S(2)}, u32[]{:S(2)}) %collective-permute-start.33) | collective-permute-done | bytes 1048608 | tf_op jit(solution)/shard_map/ppermute | solution.py:46
  263.5 2.4 fusion.24
  266.1 2.6 collective-permute-start.10
  268.7 2.3 fusion.23
  271.0 13.9 %collective-permute-done.25 = bf16[512,1024]{1,0:T(8,128)(2,1)S(1)} collective-permute-done((bf16[512,1024]{1,0:T(8,128)(2,1)S(1)}, bf16[512,1024]{1,0:T(8,128)(2,1)S(1)}, u32[]{:S(2)}, u32[]{:S(2)}) %collective-permute-start.25) | collective-permute-done | bytes 1048608 | tf_op jit(solution)/shard_map/ppermute | solution.py:46
  286.4 2.4 fusion.22
  289.6 2.4 fusion.21
  292.0 15.4 %collective-permute-done.16 = bf16[512,1024]{1,0:T(8,128)(2,1)S(1)} collective-permute-done((bf16[512,1024]{1,0:T(8,128)(2,1)S(1)}, bf16[512,1024]{1,0:T(8,128)(2,1)S(1)}, u32[]{:S(2)}, u32[]{:S(2)}) %collective-permute-start.16) | collective-permute-done | bytes 1048608 | tf_op jit(solution)/shard_map/ppermute | solution.py:46
  308.9 2.3 fusion.20
  318.2 29.6 %all_gather.3 = bf16[1024,256]{1,0:T(8,128)(2,1)S(1)} all-gather(bf16[256,256]{1,0:T(8,128)(2,1)S(1)} %pad_maximum_fusion.27), channel_id=1, replica_groups=mesh['dp'=4,'mp'=8] {'dp'}, dimensions={0}, use_global_device_ids=true | all-gather | bytes 655360 | tf_op jit(solution)/shard_map/all_gather | solution.py:283
  351.0 9.5 %fill_pages.1 = bf16[96,128,256]{2,1,0:T(8,128)(2,1)} custom-call(s32[96]{0:T(128)} %get-tuple-element.5.start_ref, s32[96]{0:T(128)} %get-tuple-element.6.count_ref, f32[1152,256]{1,0:T(8,128)} %fusion.43.rows_ref), custom_call_target="tpu_custom_call" | custom-call | flops 3145728 | bytes 7471104 | tf_op jit(solution)/shard_map/fill_pages/pallas_call | solution.py:194
  360.6 5.7 %attend.1 = bf16[256,512]{1,0:T(8,128)(2,1)} custom-call(bf16[256,512]{1,0:T(8,128)(2,1)} %copy.56.q_ref, bf16[1024,128]{1,0:T(8,128)(2,1)} %get-tuple-element.132.k_ref, bf16[1024,128]{1,0:T(8,128)(2,1)} %get-tuple-element.131.v_ref, s32[256,1]{1,0:T(8,128)} %copy.57.first_ref, s32[256,1]{1,0:T(8,128)} %iota_add_fusion.token_ref), custom_call_target="tpu_custom_call" | custom-call | flops 536870912 | bytes 1048576 | tf_op jit(solution)/shard_map/attend/pallas_call | solution.py:156
  367.0 2.0 fusion.31
  370.5 1.7 fusion.30
  372.3 2.6 collective-permute-start.45
  375.0 1.7 fusion.29
  376.7 5.6 %collective-permute-done.20 = bf16[256,1024]{1,0:T(8,128)(2,1)S(1)} collective-permute-done((bf16[256,1024]{1,0:T(8,128)(2,1)S(1)}, bf16[256,1024]{1,0:T(8,128)(2,1)S(1)}, u32[]{:S(2)}, u32[]{:S(2)}) %collective-permute-start.20) | collective-permute-done | bytes 524320 | tf_op jit(solution)/shard_map/ppermute | solution.py:46
  382.3 2.5 collective-permute-start.37
  387.0 20.9 %collective-permute-done.45 = bf16[256,1024]{1,0:T(8,128)(2,1)S(1)} collective-permute-done((bf16[256,1024]{1,0:T(8,128)(2,1)S(1)}, bf16[256,1024]{1,0:T(8,128)(2,1)S(1)}, u32[]{:S(2)}, u32[]{:S(2)}) %collective-permute-start.45) | collective-permute-done | bytes 524320 | tf_op jit(solution)/shard_map/ppermute | solution.py:46
  408.0 1.8 fusion.8
  409.8 3.0 collective-permute-start.21
  412.8 28.9 %collective-permute-done.37 = bf16[256,1024]{1,0:T(8,128)(2,1)S(1)} collective-permute-done((bf16[256,1024]{1,0:T(8,128)(2,1)S(1)}, bf16[256,1024]{1,0:T(8,128)(2,1)S(1)}, u32[]{:S(2)}, u32[]{:S(2)}) %collective-permute-start.37) | collective-permute-done | bytes 524320 | tf_op jit(solution)/shard_map/ppermute | solution.py:46
  441.7 1.8 fusion.11
  443.4 9.4 %collective-permute-done.29 = bf16[256,1024]{1,0:T(8,128)(2,1)S(1)} collective-permute-done((bf16[256,1024]{1,0:T(8,128)(2,1)S(1)}, bf16[256,1024]{1,0:T(8,128)(2,1)S(1)}, u32[]{:S(2)}, u32[]{:S(2)}) %collective-permute-start.29) | collective-permute-done | bytes 524320 | tf_op jit(solution)/shard_map/ppermute | solution.py:46
  454.2 9.8 %collective-permute-done.21 = bf16[256,1024]{1,0:T(8,128)(2,1)S(1)} collective-permute-done((bf16[256,1024]{1,0:T(8,128)(2,1)S(1)}, bf16[256,1024]{1,0:T(8,128)(2,1)S(1)}, u32[]{:S(2)}, u32[]{:S(2)}) %collective-permute-start.21) | collective-permute-done | bytes 524320 | tf_op jit(solution)/shard_map/ppermute | solution.py:46
  (421 shorter events, 81.0 us)
Async XLA Ops:
  19.2 76.3 %collective-permute-start.3 = (bf16[256,640]{1,0:T(8,128)(2,1)}, bf16[256,640]{1,0:T(8,128)(2,1)}, u32[]{:S(2)}, u32[]{:S(2)}) collective-permute-start(bf16[256,640]{1,0:T(8,128)(2,1)} %bitcast.104), channel_id=1, source_target_pairs={{0,8},{8,0},{16,24},{24,16},{1,9},{9,1},{17,25},{25,17},{2,10},{10... | collective-permute-start | bytes 983048 | tf_op jit(solution)/shard_map/ppermute | solution.py:46
  32.9 184.1 %copy-start.102 = (bf16[160,128]{1,0:T(8,128)(2,1)}, bf16[160,128]{1,0:T(8,128)(2,1)S(1)}, u32[]{:S(2)}) copy-start(bf16[160,128]{1,0:T(8,128)(2,1)S(1)} %get-tuple-element.76) | copy-start | bytes 122884
  32.9 184.1 %copy-start.104 = (bf16[160,128]{1,0:T(8,128)(2,1)}, bf16[160,128]{1,0:T(8,128)(2,1)S(1)}, u32[]{:S(2)}) copy-start(bf16[160,128]{1,0:T(8,128)(2,1)S(1)} %get-tuple-element.80) | copy-start | bytes 122884
  32.9 50.2 %collective-permute-start.2 = (bf16[160,1536]{1,0:T(8,128)(2,1)}, bf16[160,1536]{1,0:T(8,128)(2,1)}, u32[]{:S(2)}, u32[]{:S(2)}) collective-permute-start(bf16[160,1536]{1,0:T(8,128)(2,1)} %get-tuple-element.77), channel_id=1, source_target_pairs={{0,3},{1,2},{2,1},{3,0},{4,7},{5,6},{6,5},{7,4},{8,11},{9,10},{10,... | collective-permute-start | bytes 1474568 | tf_op jit(solution)/shard_map/ppermute | solution.py:46
  37.3 39.3 %collective-permute-start.14 = (bf16[256,640]{1,0:T(8,128)(2,1)}, bf16[256,640]{1,0:T(8,128)(2,1)}, u32[]{:S(2)}, u32[]{:S(2)}) collective-permute-start(bf16[256,640]{1,0:T(8,128)(2,1)} %bitcast.106), channel_id=1, source_target_pairs={{0,8},{8,0},{16,24},{24,16},{1,9},{9,1},{17,25},{25,17},{2,10},{10... | collective-permute-start | bytes 983048 | tf_op jit(solution)/shard_map/ppermute | solution.py:46
  39.7 42.2 %collective-permute-start.15 = (bf16[256,640]{1,0:T(8,128)(2,1)}, bf16[256,640]{1,0:T(8,128)(2,1)}, u32[]{:S(2)}, u32[]{:S(2)}) collective-permute-start(bf16[256,640]{1,0:T(8,128)(2,1)} %bitcast.105), channel_id=1, source_target_pairs={{0,24},{8,16},{16,8},{24,0},{1,25},{9,17},{17,9},{25,1},{2,26},{10... | collective-permute-start | bytes 983048 | tf_op jit(solution)/shard_map/ppermute | solution.py:46
  44.1 35.1 %collective-permute-start.17 = (bf16[256,640]{1,0:T(8,128)(2,1)}, bf16[256,640]{1,0:T(8,128)(2,1)}, u32[]{:S(2)}, u32[]{:S(2)}) collective-permute-start(bf16[256,640]{1,0:T(8,128)(2,1)} %bitcast.107), channel_id=1, source_target_pairs={{0,16},{8,24},{16,0},{24,8},{1,17},{9,25},{17,1},{25,9},{2,18},{10... | collective-permute-start | bytes 983048 | tf_op jit(solution)/shard_map/ppermute | solution.py:46
  76.6 16.3 %collective-permute-start.4 = (bf16[256,640]{1,0:T(8,128)(2,1)}, bf16[256,640]{1,0:T(8,128)(2,1)S(1)}, u32[]{:S(2)}, u32[]{:S(2)}) collective-permute-start(bf16[256,640]{1,0:T(8,128)(2,1)} %bitcast.109), channel_id=1, source_target_pairs={{0,24},{8,16},{16,8},{24,0},{1,25},{9,17},{17,9},{25,1},{2,26},{10... | collective-permute-start | bytes 983048 | tf_op jit(solution)/shard_map/ppermute | solution.py:46
  79.2 13.1 %collective-permute-start.1 = (bf16[160,1536]{1,0:T(8,128)(2,1)}, bf16[160,1536]{1,0:T(8,128)(2,1)S(1)}, u32[]{:S(2)}, u32[]{:S(2)}) collective-permute-start(bf16[160,1536]{1,0:T(8,128)(2,1)} %copy-done.101), channel_id=1, source_target_pairs={{0,2},{1,3},{2,0},{3,1},{4,6},{5,7},{6,4},{7,5},{8,10},{9,11},{10,... | collective-permute-start | bytes 1474568 | tf_op jit(solution)/shard_map/ppermute | solution.py:46
  81.9 10.5 %collective-permute-start = (bf16[160,1536]{1,0:T(8,128)(2,1)}, bf16[160,1536]{1,0:T(8,128)(2,1)S(1)}, u32[]{:S(2)}, u32[]{:S(2)}) collective-permute-start(bf16[160,1536]{1,0:T(8,128)(2,1)} %copy-done.100), channel_id=1, source_target_pairs={{0,1},{1,0},{2,3},{3,2},{4,5},{5,4},{6,7},{7,6},{8,9},{9,8},{10,11... | collective-permute-start | bytes 1474568 | tf_op jit(solution)/shard_map/ppermute | solution.py:46
  83.1 11.3 %collective-permute-start.6 = (bf16[256,640]{1,0:T(8,128)(2,1)S(1)}, bf16[256,640]{1,0:T(8,128)(2,1)S(1)}, u32[]{:S(2)}, u32[]{:S(2)}) collective-permute-start(bf16[256,640]{1,0:T(8,128)(2,1)S(1)} %bitcast.108), channel_id=1, source_target_pairs={{0,16},{8,24},{16,0},{24,8},{1,17},{9,25},{17,1},{25,9},{2,18},{10... | collective-permute-start | bytes 983048 | tf_op jit(solution)/shard_map/ppermute | solution.py:46
  92.3 17.0 %collective-permute-start.40 = (bf16[160,2048]{1,0:T(8,128)(2,1)S(1)}, bf16[160,2048]{1,0:T(8,128)(2,1)S(1)}, u32[]{:S(2)}, u32[]{:S(2)}) collective-permute-start(bf16[160,2048]{1,0:T(8,128)(2,1)S(1)} %copy-done.4), channel_id=1, source_target_pairs={{0,3},{1,2},{2,1},{3,0},{4,7},{5,6},{6,5},{7,4},{8,11},{9,10},{10,... | collective-permute-start | bytes 1966088 | tf_op jit(solution)/shard_map/ppermute | solution.py:46
  92.3 29.1 %collective-permute-start.39 = (bf16[160,2048]{1,0:T(8,128)(2,1)S(1)}, bf16[160,2048]{1,0:T(8,128)(2,1)S(1)}, u32[]{:S(2)}, u32[]{:S(2)}) collective-permute-start(bf16[160,2048]{1,0:T(8,128)(2,1)S(1)} %copy-done.3), channel_id=1, source_target_pairs={{0,2},{1,3},{2,0},{3,1},{4,6},{5,7},{6,4},{7,5},{8,10},{9,11},{10,... | collective-permute-start | bytes 1966088 | tf_op jit(solution)/shard_map/ppermute | solution.py:46
  92.9 30.6 %collective-permute-start.38 = (bf16[160,2048]{1,0:T(8,128)(2,1)S(1)}, bf16[160,2048]{1,0:T(8,128)(2,1)S(1)}, u32[]{:S(2)}, u32[]{:S(2)}) collective-permute-start(bf16[160,2048]{1,0:T(8,128)(2,1)S(1)} %copy-done.2), channel_id=1, source_target_pairs={{0,1},{1,0},{2,3},{3,2},{4,5},{5,4},{6,7},{7,6},{8,9},{9,8},{10,11... | collective-permute-start | bytes 1966088 | tf_op jit(solution)/shard_map/ppermute | solution.py:46
  94.4 43.0 %collective-permute-start.32 = (bf16[160,2048]{1,0:T(8,128)(2,1)S(1)}, bf16[160,2048]{1,0:T(8,128)(2,1)S(1)}, u32[]{:S(2)}, u32[]{:S(2)}) collective-permute-start(bf16[160,2048]{1,0:T(8,128)(2,1)S(1)} %copy-done.9), channel_id=1, source_target_pairs={{0,3},{1,2},{2,1},{3,0},{4,7},{5,6},{6,5},{7,4},{8,11},{9,10},{10,... | collective-permute-start | bytes 1966088 | tf_op jit(solution)/shard_map/ppermute | solution.py:46
  95.8 53.8 %collective-permute-start.31 = (bf16[160,2048]{1,0:T(8,128)(2,1)S(1)}, bf16[160,2048]{1,0:T(8,128)(2,1)S(1)}, u32[]{:S(2)}, u32[]{:S(2)}) collective-permute-start(bf16[160,2048]{1,0:T(8,128)(2,1)S(1)} %copy-done.7), channel_id=1, source_target_pairs={{0,2},{1,3},{2,0},{3,1},{4,6},{5,7},{6,4},{7,5},{8,10},{9,11},{10,... | collective-permute-start | bytes 1966088 | tf_op jit(solution)/shard_map/ppermute | solution.py:46
  109.3 42.3 %collective-permute-start.30 = (bf16[160,2048]{1,0:T(8,128)(2,1)S(1)}, bf16[160,2048]{1,0:T(8,128)(2,1)S(1)}, u32[]{:S(2)}, u32[]{:S(2)}) collective-permute-start(bf16[160,2048]{1,0:T(8,128)(2,1)S(1)} %copy-done.5), channel_id=1, source_target_pairs={{0,1},{1,0},{2,3},{3,2},{4,5},{5,4},{6,7},{7,6},{8,9},{9,8},{10,11... | collective-permute-start | bytes 1966088 | tf_op jit(solution)/shard_map/ppermute | solution.py:46
  109.4 133.2 %copy-start.37 = (bf16[160,1024]{1,0:T(8,128)(2,1)}, bf16[160,1024]{1,0:T(8,128)(2,1)S(1)}, u32[]{:S(2)}) copy-start(bf16[160,1024]{1,0:T(8,128)(2,1)S(1)} %get-tuple-element.128) | copy-start | bytes 983044
  109.4 137.2 %copy-start.15 = (bf16[160,1024]{1,0:T(8,128)(2,1)}, bf16[160,1024]{1,0:T(8,128)(2,1)S(1)}, u32[]{:S(2)}) copy-start(bf16[160,1024]{1,0:T(8,128)(2,1)S(1)} %get-tuple-element.127) | copy-start | bytes 983044
  121.5 44.0 %collective-permute-start.24 = (bf16[160,2048]{1,0:T(8,128)(2,1)S(1)}, bf16[160,2048]{1,0:T(8,128)(2,1)S(1)}, u32[]{:S(2)}, u32[]{:S(2)}) collective-permute-start(bf16[160,2048]{1,0:T(8,128)(2,1)S(1)} %copy-done.13), channel_id=1, source_target_pairs={{0,3},{1,2},{2,1},{3,0},{4,7},{5,6},{6,5},{7,4},{8,11},{9,10},{10,... | collective-permute-start | bytes 1966088 | tf_op jit(solution)/shard_map/ppermute | solution.py:46
  123.5 119.1 %copy-start.41 = (bf16[160,1024]{1,0:T(8,128)(2,1)}, bf16[160,1024]{1,0:T(8,128)(2,1)S(1)}, u32[]{:S(2)}) copy-start(bf16[160,1024]{1,0:T(8,128)(2,1)S(1)} %get-tuple-element.126) | copy-start | bytes 983044
  123.5 123.1 %copy-start.17 = (bf16[160,1024]{1,0:T(8,128)(2,1)}, bf16[160,1024]{1,0:T(8,128)(2,1)S(1)}, u32[]{:S(2)}) copy-start(bf16[160,1024]{1,0:T(8,128)(2,1)S(1)} %get-tuple-element.125) | copy-start | bytes 983044
  123.5 54.1 %collective-permute-start.23 = (bf16[160,2048]{1,0:T(8,128)(2,1)S(1)}, bf16[160,2048]{1,0:T(8,128)(2,1)S(1)}, u32[]{:S(2)}, u32[]{:S(2)}) collective-permute-start(bf16[160,2048]{1,0:T(8,128)(2,1)S(1)} %copy-done.12), channel_id=1, source_target_pairs={{0,2},{1,3},{2,0},{3,1},{4,6},{5,7},{6,4},{7,5},{8,10},{9,11},{10,... | collective-permute-start | bytes 1966088 | tf_op jit(solution)/shard_map/ppermute | solution.py:46
  125.0 117.6 %copy-start.45 = (bf16[160,1024]{1,0:T(8,128)(2,1)}, bf16[160,1024]{1,0:T(8,128)(2,1)S(1)}, u32[]{:S(2)}) copy-start(bf16[160,1024]{1,0:T(8,128)(2,1)S(1)} %get-tuple-element.124) | copy-start | bytes 983044
  125.0 121.5 %copy-start.21 = (bf16[160,1024]{1,0:T(8,128)(2,1)}, bf16[160,1024]{1,0:T(8,128)(2,1)S(1)}, u32[]{:S(2)}) copy-start(bf16[160,1024]{1,0:T(8,128)(2,1)S(1)} %get-tuple-element.123) | copy-start | bytes 983044
  137.4 41.1 %collective-permute-start.22 = (bf16[160,2048]{1,0:T(8,128)(2,1)S(1)}, bf16[160,2048]{1,0:T(8,128)(2,1)S(1)}, u32[]{:S(2)}, u32[]{:S(2)}) collective-permute-start(bf16[160,2048]{1,0:T(8,128)(2,1)S(1)} %copy-done.11), channel_id=1, source_target_pairs={{0,1},{1,0},{2,3},{3,2},{4,5},{5,4},{6,7},{7,6},{8,9},{9,8},{10,11... | collective-permute-start | bytes 1966088 | tf_op jit(solution)/shard_map/ppermute | solution.py:46
  137.5 112.1 %copy-start.43 = (bf16[160,1024]{1,0:T(8,128)(2,1)}, bf16[160,1024]{1,0:T(8,128)(2,1)S(1)}, u32[]{:S(2)}) copy-start(bf16[160,1024]{1,0:T(8,128)(2,1)S(1)} %get-tuple-element.122) | copy-start | bytes 983044
  137.5 126.0 %copy-start.19 = (bf16[160,1024]{1,0:T(8,128)(2,1)}, bf16[160,1024]{1,0:T(8,128)(2,1)S(1)}, u32[]{:S(2)}) copy-start(bf16[160,1024]{1,0:T(8,128)(2,1)S(1)} %get-tuple-element.121) | copy-start | bytes 983044
  149.5 44.0 %collective-permute-start.13 = (bf16[160,2048]{1,0:T(8,128)(2,1)S(1)}, bf16[160,2048]{1,0:T(8,128)(2,1)S(1)}, u32[]{:S(2)}, u32[]{:S(2)}) collective-permute-start(bf16[160,2048]{1,0:T(8,128)(2,1)S(1)} %copy-done.8), channel_id=1, source_target_pairs={{0,3},{1,2},{2,1},{3,0},{4,7},{5,6},{6,5},{7,4},{8,11},{9,10},{10,... | collective-permute-start | bytes 1966088 | tf_op jit(solution)/shard_map/ppermute | solution.py:46
  151.6 111.9 %copy-start.23 = (bf16[160,1024]{1,0:T(8,128)(2,1)}, bf16[160,1024]{1,0:T(8,128)(2,1)S(1)}, u32[]{:S(2)}) copy-start(bf16[160,1024]{1,0:T(8,128)(2,1)S(1)} %get-tuple-element.119) | copy-start | bytes 983044
  151.6 54.1 %collective-permute-start.12 = (bf16[160,2048]{1,0:T(8,128)(2,1)S(1)}, bf16[160,2048]{1,0:T(8,128)(2,1)S(1)}, u32[]{:S(2)}, u32[]{:S(2)}) collective-permute-start(bf16[160,2048]{1,0:T(8,128)(2,1)S(1)} %copy-done.10), channel_id=1, source_target_pairs={{0,2},{1,3},{2,0},{3,1},{4,6},{5,7},{6,4},{7,5},{8,10},{9,11},{10,... | collective-permute-start | bytes 1966088 | tf_op jit(solution)/shard_map/ppermute | solution.py:46
  153.1 110.4 %copy-start.27 = (bf16[160,1024]{1,0:T(8,128)(2,1)}, bf16[160,1024]{1,0:T(8,128)(2,1)S(1)}, u32[]{:S(2)}) copy-start(bf16[160,1024]{1,0:T(8,128)(2,1)S(1)} %get-tuple-element.117) | copy-start | bytes 983044
  165.5 43.9 %collective-permute-start.11 = (bf16[160,2048]{1,0:T(8,128)(2,1)S(1)}, bf16[160,2048]{1,0:T(8,128)(2,1)S(1)}, u32[]{:S(2)}, u32[]{:S(2)}) collective-permute-start(bf16[160,2048]{1,0:T(8,128)(2,1)S(1)} %copy-done.6), channel_id=1, source_target_pairs={{0,1},{1,0},{2,3},{3,2},{4,5},{5,4},{6,7},{7,6},{8,9},{9,8},{10,11... | collective-permute-start | bytes 1966088 | tf_op jit(solution)/shard_map/ppermute | solution.py:46
  165.5 103.1 %copy-start.49 = (bf16[160,1024]{1,0:T(8,128)(2,1)}, bf16[160,1024]{1,0:T(8,128)(2,1)S(1)}, u32[]{:S(2)}) copy-start(bf16[160,1024]{1,0:T(8,128)(2,1)S(1)} %get-tuple-element.116) | copy-start | bytes 983044
  165.6 120.8 %copy-start.25 = (bf16[160,1024]{1,0:T(8,128)(2,1)}, bf16[160,1024]{1,0:T(8,128)(2,1)S(1)}, u32[]{:S(2)}) copy-start(bf16[160,1024]{1,0:T(8,128)(2,1)S(1)} %get-tuple-element.115) | copy-start | bytes 983044
  177.6 34.7 %collective-permute-start.8 = (bf16[512,768]{1,0:T(8,128)(2,1)S(1)}, bf16[512,768]{1,0:T(8,128)(2,1)S(1)}, u32[]{:S(2)}, u32[]{:S(2)}) collective-permute-start(bf16[512,768]{1,0:T(8,128)(2,1)S(1)} %convolution_convert_fusion.8), channel_id=1, source_target_pairs={{0,16},{8,24},{16,0},{24,8},{1,17},{9,25},{17,1},{25,9},{2,18},{10... | collective-permute-start | bytes 2359304 | tf_op jit(solution)/shard_map/ppermute | solution.py:46
  178.5 107.9 %copy-start.29 = (bf16[160,1024]{1,0:T(8,128)(2,1)}, bf16[160,1024]{1,0:T(8,128)(2,1)S(1)}, u32[]{:S(2)}) copy-start(bf16[160,1024]{1,0:T(8,128)(2,1)S(1)} %get-tuple-element.113) | copy-start | bytes 983044
  178.5 37.3 %collective-permute-start.5 = (bf16[512,768]{1,0:T(8,128)(2,1)S(1)}, bf16[512,768]{1,0:T(8,128)(2,1)S(1)}, u32[]{:S(2)}, u32[]{:S(2)}) collective-permute-start(bf16[512,768]{1,0:T(8,128)(2,1)S(1)} %convolution_convert_fusion.9), channel_id=1, source_target_pairs={{0,8},{8,0},{16,24},{24,16},{1,9},{9,1},{17,25},{25,17},{2,10},{10... | collective-permute-start | bytes 2359304 | tf_op jit(solution)/shard_map/ppermute | solution.py:46
  179.8 106.6 %copy-start.33 = (bf16[160,1024]{1,0:T(8,128)(2,1)}, bf16[160,1024]{1,0:T(8,128)(2,1)S(1)}, u32[]{:S(2)}) copy-start(bf16[160,1024]{1,0:T(8,128)(2,1)S(1)} %get-tuple-element.111) | copy-start | bytes 983044
  193.6 48.0 %collective-permute-start.43 = (bf16[512,1024]{1,0:T(8,128)(2,1)S(1)}, bf16[512,1024]{1,0:T(8,128)(2,1)S(1)}, u32[]{:S(2)}, u32[]{:S(2)}) collective-permute-start(bf16[512,1024]{1,0:T(8,128)(2,1)S(1)} %convolution_convert_fusion), channel_id=1, source_target_pairs={{0,16},{8,24},{16,0},{24,8},{1,17},{9,25},{17,1},{25,9},{2,18},{10... | collective-permute-start | bytes 3145736 | tf_op jit(solution)/shard_map/ppermute | solution.py:46
  194.2 114.7 %copy-start.31 = (bf16[160,1024]{1,0:T(8,128)(2,1)}, bf16[160,1024]{1,0:T(8,128)(2,1)S(1)}, u32[]{:S(2)}) copy-start(bf16[160,1024]{1,0:T(8,128)(2,1)S(1)} %get-tuple-element.109) | copy-start | bytes 983044
  205.6 39.3 %collective-permute-start.41 = (bf16[512,1024]{1,0:T(8,128)(2,1)S(1)}, bf16[512,1024]{1,0:T(8,128)(2,1)S(1)}, u32[]{:S(2)}, u32[]{:S(2)}) collective-permute-start(bf16[512,1024]{1,0:T(8,128)(2,1)S(1)} %convolution_convert_fusion.1), channel_id=1, source_target_pairs={{0,8},{8,0},{16,24},{24,16},{1,9},{9,1},{17,25},{25,17},{2,10},{10... | collective-permute-start | bytes 3145736 | tf_op jit(solution)/shard_map/ppermute | solution.py:46
  207.2 101.7 %copy-start.35 = (bf16[160,1024]{1,0:T(8,128)(2,1)}, bf16[160,1024]{1,0:T(8,128)(2,1)S(1)}, u32[]{:S(2)}) copy-start(bf16[160,1024]{1,0:T(8,128)(2,1)S(1)} %get-tuple-element.107) | copy-start | bytes 983044
  209.4 39.5 %collective-permute-start.35 = (bf16[512,1024]{1,0:T(8,128)(2,1)S(1)}, bf16[512,1024]{1,0:T(8,128)(2,1)S(1)}, u32[]{:S(2)}, u32[]{:S(2)}) collective-permute-start(bf16[512,1024]{1,0:T(8,128)(2,1)S(1)} %convolution_convert_fusion.2), channel_id=1, source_target_pairs={{0,16},{8,24},{16,0},{24,8},{1,17},{9,25},{17,1},{25,9},{2,18},{10... | collective-permute-start | bytes 3145736 | tf_op jit(solution)/shard_map/ppermute | solution.py:46
  213.8 26.1 %collective-permute-start.9 = (bf16[256,768]{1,0:T(8,128)(2,1)S(1)}, bf16[256,768]{1,0:T(8,128)(2,1)S(1)}, u32[]{:S(2)}, u32[]{:S(2)}) collective-permute-start(bf16[256,768]{1,0:T(8,128)(2,1)S(1)} %fusion.37), channel_id=1, source_target_pairs={{0,8},{8,0},{16,24},{24,16},{1,9},{9,1},{17,25},{25,17},{2,10},{10... | collective-permute-start | bytes 1179656 | tf_op jit(solution)/shard_map/ppermute | solution.py:46
  215.8 46.6 %collective-permute-start.33 = (bf16[512,1024]{1,0:T(8,128)(2,1)S(1)}, bf16[512,1024]{1,0:T(8,128)(2,1)S(1)}, u32[]{:S(2)}, u32[]{:S(2)}) collective-permute-start(bf16[512,1024]{1,0:T(8,128)(2,1)S(1)} %convolution_convert_fusion.3), channel_id=1, source_target_pairs={{0,8},{8,0},{16,24},{24,16},{1,9},{9,1},{17,25},{25,17},{2,10},{10... | collective-permute-start | bytes 3145736 | tf_op jit(solution)/shard_map/ppermute | solution.py:46
  240.0 26.1 %collective-permute-start.27 = (bf16[512,1024]{1,0:T(8,128)(2,1)S(1)}, bf16[512,1024]{1,0:T(8,128)(2,1)S(1)}, u32[]{:S(2)}, u32[]{:S(2)}) collective-permute-start(bf16[512,1024]{1,0:T(8,128)(2,1)S(1)} %convolution_convert_fusion.4), channel_id=1, source_target_pairs={{0,16},{8,24},{16,0},{24,8},{1,17},{9,25},{17,1},{25,9},{2,18},{10... | collective-permute-start | bytes 3145736 | tf_op jit(solution)/shard_map/ppermute | solution.py:46
  241.6 43.3 %collective-permute-start.25 = (bf16[512,1024]{1,0:T(8,128)(2,1)S(1)}, bf16[512,1024]{1,0:T(8,128)(2,1)S(1)}, u32[]{:S(2)}, u32[]{:S(2)}) collective-permute-start(bf16[512,1024]{1,0:T(8,128)(2,1)S(1)} %convolution_convert_fusion.5), channel_id=1, source_target_pairs={{0,8},{8,0},{16,24},{24,16},{1,9},{9,1},{17,25},{25,17},{2,10},{10... | collective-permute-start | bytes 3145736 | tf_op jit(solution)/shard_map/ppermute | solution.py:46
  244.9 43.8 %collective-permute-start.19 = (bf16[512,1024]{1,0:T(8,128)(2,1)S(1)}, bf16[512,1024]{1,0:T(8,128)(2,1)S(1)}, u32[]{:S(2)}, u32[]{:S(2)}) collective-permute-start(bf16[512,1024]{1,0:T(8,128)(2,1)S(1)} %convolution_convert_fusion.6), channel_id=1, source_target_pairs={{0,16},{8,24},{16,0},{24,8},{1,17},{9,25},{17,1},{25,9},{2,18},{10... | collective-permute-start | bytes 3145736 | tf_op jit(solution)/shard_map/ppermute | solution.py:46
  248.9 58.5 %collective-permute-start.16 = (bf16[512,1024]{1,0:T(8,128)(2,1)S(1)}, bf16[512,1024]{1,0:T(8,128)(2,1)S(1)}, u32[]{:S(2)}, u32[]{:S(2)}) collective-permute-start(bf16[512,1024]{1,0:T(8,128)(2,1)S(1)} %convolution_convert_fusion.7), channel_id=1, source_target_pairs={{0,8},{8,0},{16,24},{24,16},{1,9},{9,1},{17,25},{25,17},{2,10},{10... | collective-permute-start | bytes 3145736 | tf_op jit(solution)/shard_map/ppermute | solution.py:46
  262.4 48.8 %collective-permute-start.7 = (bf16[256,768]{1,0:T(8,128)(2,1)S(1)}, bf16[256,768]{1,0:T(8,128)(2,1)S(1)}, u32[]{:S(2)}, u32[]{:S(2)}) collective-permute-start(bf16[256,768]{1,0:T(8,128)(2,1)S(1)} %fusion.35), channel_id=1, source_target_pairs={{0,16},{8,24},{16,0},{24,8},{1,17},{9,25},{17,1},{25,9},{2,18},{10... | collective-permute-start | bytes 1179656 | tf_op jit(solution)/shard_map/ppermute | solution.py:46
  266.1 45.7 %collective-permute-start.10 = (bf16[256,768]{1,0:T(8,128)(2,1)S(1)}, bf16[256,768]{1,0:T(8,128)(2,1)S(1)}, u32[]{:S(2)}, u32[]{:S(2)}) collective-permute-start(bf16[256,768]{1,0:T(8,128)(2,1)S(1)} %fusion.36), channel_id=1, source_target_pairs={{0,4},{1,5},{2,6},{3,7},{4,0},{5,1},{6,2},{7,3},{8,12},{9,13},{10,... | collective-permute-start | bytes 1179656 | tf_op jit(solution)/shard_map/ppermute | solution.py:46
  284.9 81.4 %collective-permute-start.44 = (bf16[256,1024]{1,0:T(8,128)(2,1)}, bf16[256,1024]{1,0:T(8,128)(2,1)}, u32[]{:S(2)}, u32[]{:S(2)}) collective-permute-start(bf16[256,1024]{1,0:T(8,128)(2,1)} %fusion.27), channel_id=1, source_target_pairs={{0,8},{8,0},{16,24},{24,16},{1,9},{9,1},{17,25},{25,17},{2,10},{10... | collective-permute-start | bytes 1572872 | tf_op jit(solution)/shard_map/ppermute | solution.py:46
  288.8 96.8 %collective-permute-start.42 = (bf16[256,1024]{1,0:T(8,128)(2,1)}, bf16[256,1024]{1,0:T(8,128)(2,1)}, u32[]{:S(2)}, u32[]{:S(2)}) collective-permute-start(bf16[256,1024]{1,0:T(8,128)(2,1)} %fusion.26), channel_id=1, source_target_pairs={{0,16},{8,24},{16,0},{24,8},{1,17},{9,25},{17,1},{25,9},{2,18},{10... | collective-permute-start | bytes 1572872 | tf_op jit(solution)/shard_map/ppermute | solution.py:46
  307.4 61.7 %collective-permute-start.36 = (bf16[256,1024]{1,0:T(8,128)(2,1)}, bf16[256,1024]{1,0:T(8,128)(2,1)}, u32[]{:S(2)}, u32[]{:S(2)}) collective-permute-start(bf16[256,1024]{1,0:T(8,128)(2,1)} %fusion.25), channel_id=1, source_target_pairs={{0,8},{8,0},{16,24},{24,16},{1,9},{9,1},{17,25},{25,17},{2,10},{10... | collective-permute-start | bytes 1572872 | tf_op jit(solution)/shard_map/ppermute | solution.py:46
  311.2 98.6 %collective-permute-start.34 = (bf16[256,1024]{1,0:T(8,128)(2,1)}, bf16[256,1024]{1,0:T(8,128)(2,1)}, u32[]{:S(2)}, u32[]{:S(2)}) collective-permute-start(bf16[256,1024]{1,0:T(8,128)(2,1)} %fusion.24), channel_id=1, source_target_pairs={{0,16},{8,24},{16,0},{24,8},{1,17},{9,25},{17,1},{25,9},{2,18},{10... | collective-permute-start | bytes 1572872 | tf_op jit(solution)/shard_map/ppermute | solution.py:46
  311.7 60.5 %collective-permute-start.28 = (bf16[256,1024]{1,0:T(8,128)(2,1)}, bf16[256,1024]{1,0:T(8,128)(2,1)}, u32[]{:S(2)}, u32[]{:S(2)}) collective-permute-start(bf16[256,1024]{1,0:T(8,128)(2,1)} %fusion.23), channel_id=1, source_target_pairs={{0,8},{8,0},{16,24},{24,16},{1,9},{9,1},{17,25},{25,17},{2,10},{10... | collective-permute-start | bytes 1572872 | tf_op jit(solution)/shard_map/ppermute | solution.py:46
  366.3 77.1 %collective-permute-start.26 = (bf16[256,1024]{1,0:T(8,128)(2,1)S(1)}, bf16[256,1024]{1,0:T(8,128)(2,1)S(1)}, u32[]{:S(2)}, u32[]{:S(2)}) collective-permute-start(bf16[256,1024]{1,0:T(8,128)(2,1)S(1)} %copy-done.128), channel_id=1, source_target_pairs={{0,16},{8,24},{16,0},{24,8},{1,17},{9,25},{17,1},{25,9},{2,18},{10... | collective-permute-start | bytes 1572872 | tf_op jit(solution)/shard_map/ppermute | solution.py:46
  369.0 13.3 %collective-permute-start.20 = (bf16[256,1024]{1,0:T(8,128)(2,1)S(1)}, bf16[256,1024]{1,0:T(8,128)(2,1)S(1)}, u32[]{:S(2)}, u32[]{:S(2)}) collective-permute-start(bf16[256,1024]{1,0:T(8,128)(2,1)S(1)} %copy-done.129), channel_id=1, source_target_pairs={{0,8},{8,0},{16,24},{24,16},{1,9},{9,1},{17,25},{25,17},{2,10},{10... | collective-permute-start | bytes 1572872 | tf_op jit(solution)/shard_map/ppermute | solution.py:46
  372.3 35.6 %collective-permute-start.45 = (bf16[256,1024]{1,0:T(8,128)(2,1)S(1)}, bf16[256,1024]{1,0:T(8,128)(2,1)S(1)}, u32[]{:S(2)}, u32[]{:S(2)}) collective-permute-start(bf16[256,1024]{1,0:T(8,128)(2,1)S(1)} %fusion.31), channel_id=1, source_target_pairs={{0,4},{1,5},{2,6},{3,7},{4,0},{5,1},{6,2},{7,3},{8,12},{9,13},{10,... | collective-permute-start | bytes 1572872 | tf_op jit(solution)/shard_map/ppermute | solution.py:46
  382.3 59.3 %collective-permute-start.37 = (bf16[256,1024]{1,0:T(8,128)(2,1)S(1)}, bf16[256,1024]{1,0:T(8,128)(2,1)S(1)}, u32[]{:S(2)}, u32[]{:S(2)}) collective-permute-start(bf16[256,1024]{1,0:T(8,128)(2,1)S(1)} %fusion.30), channel_id=1, source_target_pairs={{0,4},{1,5},{2,6},{3,7},{4,0},{5,1},{6,2},{7,3},{8,12},{9,13},{10,... | collective-permute-start | bytes 1572872 | tf_op jit(solution)/shard_map/ppermute | solution.py:46
  385.6 68.5 %collective-permute-start.18 = (bf16[256,1024]{1,0:T(8,128)(2,1)S(1)}, bf16[256,1024]{1,0:T(8,128)(2,1)S(1)}, u32[]{:S(2)}, u32[]{:S(2)}) collective-permute-start(bf16[256,1024]{1,0:T(8,128)(2,1)S(1)} %copy-done.127), channel_id=1, source_target_pairs={{0,16},{8,24},{16,0},{24,8},{1,17},{9,25},{17,1},{25,9},{2,18},{10... | collective-permute-start | bytes 1572872 | tf_op jit(solution)/shard_map/ppermute | solution.py:46
  407.9 44.9 %collective-permute-start.29 = (bf16[256,1024]{1,0:T(8,128)(2,1)S(1)}, bf16[256,1024]{1,0:T(8,128)(2,1)S(1)}, u32[]{:S(2)}, u32[]{:S(2)}) collective-permute-start(bf16[256,1024]{1,0:T(8,128)(2,1)S(1)} %fusion.29), channel_id=1, source_target_pairs={{0,4},{1,5},{2,6},{3,7},{4,0},{5,1},{6,2},{7,3},{8,12},{9,13},{10,... | collective-permute-start | bytes 1572872 | tf_op jit(solution)/shard_map/ppermute | solution.py:46
  409.8 54.2 %collective-permute-start.21 = (bf16[256,1024]{1,0:T(8,128)(2,1)S(1)}, bf16[256,1024]{1,0:T(8,128)(2,1)S(1)}, u32[]{:S(2)}, u32[]{:S(2)}) collective-permute-start(bf16[256,1024]{1,0:T(8,128)(2,1)S(1)} %fusion.28), channel_id=1, source_target_pairs={{0,4},{1,5},{2,6},{3,7},{4,0},{5,1},{6,2},{7,3},{8,12},{9,13},{10,... | collective-permute-start | bytes 1572872 | tf_op jit(solution)/shard_map/ppermute | solution.py:46
  (113 other events, 2313.1 us)
